TPU v7x, 32 devices: a whole 2x2x4 slice. The times are simulated.
32 devices in a mesh: batch: 8 (over y, x, core), chan: 4 (over z).
Axes of the slice: x: 2, y: 2, z: 4, core: 2. Of those that a mesh axis runs over, the one named last changes fastest.
Arguments:
- fine_inputs: bfloat16 [8, 32, 32, 512], P('batch'), may hold values from -6 to 6
- fine_upstream: bfloat16 [8, 32, 32, 512], P('batch', None, None, 'chan'), may hold values from -6 to 6
- fine_bank: bfloat16 [8, 9, 512, 512], P(None, None, 'batch', 'chan'), may hold values from -0.09375 to 0.09375
- fine_coefs: float32 [8, 8], replicated, may hold values from 0 to 1, as said below
- coarse_inputs: bfloat16 [8, 16, 16, 512], P('batch'), may hold values from -6 to 6
- coarse_upstream: bfloat16 [8, 16, 16, 512], P('batch', None, None, 'chan'), may hold values from -6 to 6
- coarse_bank: bfloat16 [8, 9, 512, 512], P(None, None, 'batch', 'chan'), may hold values from -0.09375 to 0.09375
- coarse_coefs: float32 [8, 8], replicated, may hold values from 0 to 1, as said below
Outputs:
- fine_delta: bfloat16 [8, 32, 32, 512], P('batch', None, None, 'chan')
- fine_update: float32 [8, 9, 512, 512], P(None, None, 'batch', 'chan')
- fine_logit: float32 [8, 8], P('batch')
- coarse_delta: bfloat16 [8, 16, 16, 512], P('batch', None, None, 'chan')
- coarse_update: float32 [8, 9, 512, 512], P(None, None, 'batch', 'chan')
- coarse_logit: float32 [8, 8], P('batch')
Inputs may be any that keep to these rules, and one draw needn't show every extreme that they name: Each row of fine_coefs is a softmax: positive entries that sum to one. Each row of coarse_coefs is a softmax: positive entries that sum to one.
All inputs are finite; a program needn't handle non-finite values.
Results may differ from a plain program's by a relative error of at most 0.01.
Values may be sent and summed in bfloat16 or wider, within the bound.
No kernel may reach another device: no remote copies, remote signals or barrier semaphores. Data moves between devices by JAX's collectives and lax.ppermute only.
A program may use at most 128 MiB of HBM per device.

v0:
```python
import jax
import jax.numpy as jnp
from jax import lax
from jax.sharding import PartitionSpec as P

BANKS = 8
FINE_SIDE = 32
COARSE_SIDE = 16
HIGH = lax.Precision.HIGHEST


def shifted(padded, row_shift, col_shift, side):
    window = padded[:, row_shift : row_shift + side, col_shift : col_shift + side, :]
    return window.reshape(window.shape[0], side * side, window.shape[3])


def local_grads(inputs, upstream, kernels, side):
    samples_here = inputs.shape[0]
    pad_in = jnp.pad(inputs, ((0, 0), (1, 1), (1, 1), (0, 0)))
    pad_up = jnp.pad(upstream, ((0, 0), (1, 1), (1, 1), (0, 0)))
    flat_up = upstream.reshape(samples_here, side * side, upstream.shape[3])
    delta = jnp.zeros((samples_here, side * side, inputs.shape[3]), jnp.float32)
    grad_taps = []
    for row_shift in range(3):
        for col_shift in range(3):
            tap = 3 * row_shift + col_shift
            window_in = shifted(pad_in, row_shift, col_shift, side)
            window_up = shifted(pad_up, 2 - row_shift, 2 - col_shift, side)
            grad_taps.append(
                jnp.einsum("bpc,bpo->bco", window_in, flat_up, preferred_element_type=jnp.float32)
                / side
            )
            delta = delta + jnp.einsum(
                "bpo,bco->bpc", window_up, kernels[:, tap], preferred_element_type=jnp.float32
            )
    return (delta.reshape(samples_here, side, side, inputs.shape[3]), jnp.stack(grad_taps, axis=1))


def one_layer(inputs, upstream, bank_part, coefs, side):
    flat_bank = bank_part.reshape(BANKS, -1).astype(jnp.float32)
    mixed_all = jnp.dot(coefs, flat_bank, precision=HIGH)
    mixed_all = mixed_all.reshape((coefs.shape[0],) + bank_part.shape[1:]).astype(jnp.bfloat16)
    kernels = lax.all_to_all(mixed_all, "batch", split_axis=0, concat_axis=2, tiled=True)
    delta, kernel_grad = local_grads(inputs, upstream, kernels, side)
    delta_total = lax.psum(delta.astype(jnp.bfloat16), "chan").astype(jnp.float32)
    width = delta.shape[3] // lax.axis_size("chan")
    delta_part = lax.dynamic_slice_in_dim(delta_total, lax.axis_index("chan") * width, width, 3)
    moved = lax.all_to_all(
        kernel_grad.astype(jnp.bfloat16), "batch", split_axis=2, concat_axis=0, tiled=True
    ).astype(kernel_grad.dtype)
    flat_grads = moved.reshape(moved.shape[0], -1)
    update = jnp.dot(coefs.T, flat_grads, precision=HIGH).reshape(bank_part.shape)
    dcoef_part = lax.dot_general(flat_grads, flat_bank, (((1,), (1,)), ((), ())), precision=HIGH)
    return (delta_part.astype(jnp.bfloat16), update, dcoef_part)


def logit_grads(coefs, totals, samples_here):
    first_row = lax.axis_index("batch") * samples_here
    own_coefs = lax.dynamic_slice_in_dim(coefs, first_row, samples_here, 0)
    own_totals = lax.dynamic_slice_in_dim(totals, first_row, samples_here, 0)
    return own_coefs * (own_totals - jnp.sum(own_coefs * own_totals, axis=1, keepdims=True))


def per_device(
    fine_inputs,
    fine_upstream,
    fine_bank,
    fine_coefs,
    coarse_inputs,
    coarse_upstream,
    coarse_bank,
    coarse_coefs,
):
    fine_delta, fine_update, fine_partial = one_layer(
        fine_inputs, fine_upstream, fine_bank, fine_coefs, FINE_SIDE
    )
    coarse_delta, coarse_update, coarse_partial = one_layer(
        coarse_inputs, coarse_upstream, coarse_bank, coarse_coefs, COARSE_SIDE
    )
    fine_total, coarse_total = lax.psum((fine_partial, coarse_partial), ("batch", "chan"))
    samples_here = fine_inputs.shape[0]
    fine_logit = logit_grads(fine_coefs, fine_total, samples_here)
    coarse_logit = logit_grads(coarse_coefs, coarse_total, samples_here)
    return (fine_delta, fine_update, fine_logit, coarse_delta, coarse_update, coarse_logit)


def solution(mesh):
    return jax.shard_map(
        per_device,
        mesh=mesh,
        in_specs=(
            P("batch", None, None, None),
            P("batch", None, None, "chan"),
            P(None, None, "batch", "chan"),
            P(),
            P("batch", None, None, None),
            P("batch", None, None, "chan"),
            P(None, None, "batch", "chan"),
            P(),
        ),
        out_specs=(
            P("batch", None, None, "chan"),
            P(None, None, "batch", "chan"),
            P("batch", None),
            P("batch", None, None, "chan"),
            P(None, None, "batch", "chan"),
            P("batch", None),
        ),
        check_vma=False,
    )
```

profile of v0, /device:TPU:10, one launch (start us, length us, event | category | flops | bytes accessed | tf_op | source)
XLA Modules:
  0.0 182.0 jit_solution(2190526697358805732)
XLA Ops:
  7.2 2.0 %copy.47 = bf16[1,8,576,128]{3,1,2,0:T(8,128)(2,1)S(1)} copy(bf16[1,8,576,128]{3,2,1,0:T(8,128)(2,1)} %bitcast.542) | data formatting | bytes 2359296
  9.2 1.1 convolution_convert_fusion.1
  10.3 1.3 copy.24
  11.6 4.4 %all-to-all-start = ((bf16[8,9,64,128]{3,2,1,0:T(8,128)(2,1)}), bf16[8,9,64,128]{3,2,1,0:T(8,128)(2,1)S(1)}, u32[]{:S(2)}, u32[]{:S(2)}) async-start(bf16[8,9,64,128]{3,2,1,0:T(8,128)(2,1)} %copy.24), calls=%async_computation | async-start | bytes 2359296 | tf_op jit(solution)/shard_map/all_to_all | solution.py:43
  16.0 0.8 copy.46
  24.5 1.1 convolution_convert_fusion
  25.9 1.3 copy.29
  27.2 2.2 %copy.27 = bf16[1,9,512,128]{3,1,0,2:T(8,128)(2,1)} copy(bf16[1,9,512,128]{3,2,1,0:T(8,128)(2,1)S(1)} %fusion.62) | data formatting | bytes 2359296 | tf_op jit(solution)/shard_map/stack | solution.py:36
  29.5 1.3 fusion.48
  31.4 2.2 %copy.31 = bf16[1,9,512,128]{3,1,0,2:T(8,128)(2,1)} copy(bf16[1,9,512,128]{3,2,1,0:T(8,128)(2,1)S(1)} %fusion.44) | data formatting | bytes 2359296 | tf_op jit(solution)/shard_map/stack | solution.py:36
  33.6 0.8 pad_slice_fusion.24
  34.4 1.2 pad_slice_fusion.16
  35.6 4.3 %all-to-all-start.1 = ((bf16[1,9,512,128]{3,1,0,2:T(8,128)(2,1)}), bf16[1,9,512,128]{3,1,0,2:T(8,128)(2,1)}, u32[]{:S(2)}, u32[]{:S(2)}) async-start(bf16[1,9,512,128]{3,1,0,2:T(8,128)(2,1)} %copy.27), calls=%async_computation.1 | async-start | bytes 4194304 | tf_op jit(solution)/shard_map/all_to_all | solution.py:48
  40.5 1.8 fusion.124
  42.2 1.7 fusion.125
  44.0 1.7 fusion.126
  45.7 19.4 %all-to-all-done.1 = bf16[1,9,512,128]{3,1,0,2:T(8,128)(2,1)} async-done(((bf16[1,9,512,128]{3,1,0,2:T(8,128)(2,1)}), bf16[1,9,512,128]{3,1,0,2:T(8,128)(2,1)}, u32[]{:S(2)}, u32[]{:S(2)}) %all-to-all-start.1) | async-done | bytes 1179680 | tf_op jit(solution)/shard_map/all_to_all | solution.py:48
  65.1 5.7 %all-to-all-start.2 = ((bf16[8,9,64,128]{3,2,1,0:T(8,128)(2,1)}), bf16[8,9,64,128]{3,2,1,0:T(8,128)(2,1)}, u32[]{:S(2)}, u32[]{:S(2)}) async-start(bf16[8,9,64,128]{3,2,1,0:T(8,128)(2,1)} %copy.29), calls=%async_computation.2 | async-start | bytes 2359296 | tf_op jit(solution)/shard_map/all_to_all | solution.py:43
  70.8 3.0 %copy.49 = bf16[1,9,8,64,128]{4,3,1,2,0:T(8,128)(2,1)} copy(bf16[1,9,8,64,128]{4,1,3,2,0:T(8,128)(2,1)} %bitcast.57) | data formatting | bytes 2359296 | tf_op jit(solution)/shard_map/all_to_all | solution.py:48
  73.8 1.8 reshape.837
  75.5 2.9 %fusion.127 = f32[1024,512]{1,0:T(8,128)} fusion(bf16[1024,128]{1,0:T(8,128)(2,1)} %bitcast.554, bf16[1,9,512,128]{3,2,1,0:T(8,128)(2,1)} %bitcast.526), kind=kOutput, calls=%fused_computation.192 | convolution fusion | flops 134217728 | bytes 2490368 | tf_op jit(solution)/shard_map/bpo,bco->bpc/dot_general | solution.py:33
  78.4 2.7 %fusion.128 = f32[1024,512]{1,0:T(8,128)} fusion(bf16[1024,128]{1,0:T(8,128)(2,1)S(1)} %bitcast.553, bf16[1,9,512,128]{3,2,1,0:T(8,128)(2,1)} %bitcast.527), kind=kOutput, calls=%fused_computation.194 | convolution fusion | flops 134217728 | bytes 2490368 | tf_op jit(solution)/shard_map/bpo,bco->bpc/dot_general | solution.py:33
  81.1 2.7 %fusion.130 = f32[1024,512]{1,0:T(8,128)} fusion(bf16[1024,128]{1,0:T(8,128)(2,1)S(1)} %bitcast.552, bf16[1,9,512,128]{3,2,1,0:T(8,128)(2,1)} %bitcast.528), kind=kOutput, calls=%fused_computation.198 | convolution fusion | flops 134217728 | bytes 2490368 | tf_op jit(solution)/shard_map/bpo,bco->bpc/dot_general | solution.py:33
  83.8 2.7 %fusion.129 = f32[1024,512]{1,0:T(8,128)} fusion(bf16[1024,128]{1,0:T(8,128)(2,1)S(1)} %bitcast.551, bf16[1,9,512,128]{3,2,1,0:T(8,128)(2,1)} %bitcast.529), kind=kOutput, calls=%fused_computation.196 | convolution fusion | flops 134217728 | bytes 2490368 | tf_op jit(solution)/shard_map/bpo,bco->bpc/dot_general | solution.py:33
  86.5 5.4 %all-to-all-start.3 = ((bf16[1,9,512,128]{3,1,0,2:T(8,128)(2,1)}), bf16[1,9,512,128]{3,1,0,2:T(8,128)(2,1)}, u32[]{:S(2)}, u32[]{:S(2)}) async-start(bf16[1,9,512,128]{3,1,0,2:T(8,128)(2,1)} %copy.31), calls=%async_computation.3 | async-start | bytes 4194304 | tf_op jit(solution)/shard_map/all_to_all | solution.py:48
  91.9 1.5 copy.30
  93.5 1.1 fusion.122
  94.6 1.1 convolution_add_fusion.6
  95.8 1.2 convolution_add_fusion.5
  97.0 1.2 convolution_add_fusion.4
  98.5 1.2 convolution_add_fusion.3
  100.2 1.9 %fusion.6 = bf16[256,512]{1,0:T(8,128)(2,1)} fusion(f32[256,512]{1,0:T(8,128)S(1)} %convolution_add_fusion.1, bf16[256,128]{1,0:T(8,128)(2,1)} %bitcast.567, bf16[1,9,512,128]{3,2,1,0:T(8,128)(2,1)S(1)} %bitcast.539), kind=kOutput, calls=%fused_computation.25 | convolution fusion | flops 33816576 | bytes 983040 | tf_op jit(solution)/shard_map/bpo,bco->bpc/dot_general | solution.py:33
  102.2 3.8 %fusion.4 = bf16[1024,512]{1,0:T(8,128)(2,1)} fusion(f32[1024,512]{1,0:T(8,128)S(1)} %fusion.123, f32[1024,512]{1,0:T(8,128)S(1)} %copy-done, f32[1024,512]{1,0:T(8,128)S(1)} %copy-done.1, f32[512,1024]{0,1:T(8,128)S(1)} %copy-done.2, f32[1024,512]{1,0:T(8,128)S(1)} %copy-done.3, f32[1024,512]{1,0:T(8,128)S(1)} %copy-done.4, f32[1024,512]{1,0:T(8,128)S(1)} %copy-done.5, ...), kind=kOutput, calls=%fused_computation.5 | convolution fusion | flops 138936320 | bytes 18219008 | tf_op jit(solution)/shard_map/bpo,bco->bpc/dot_general | solution.py:33
  106.0 1.2 fusion.160
  107.2 1.8 %copy.33 = f32[8,9,64,128]{3,2,1,0:T(8,128)} copy(f32[8,9,64,128]{3,0,2,1:T(8,128)S(1)} %bitcast.520) | data formatting | bytes 4718592
  109.0 8.1 %all-to-all-done.3 = bf16[1,9,512,128]{3,1,0,2:T(8,128)(2,1)} async-done(((bf16[1,9,512,128]{3,1,0,2:T(8,128)(2,1)}), bf16[1,9,512,128]{3,1,0,2:T(8,128)(2,1)}, u32[]{:S(2)}, u32[]{:S(2)}) %all-to-all-start.3) | async-done | bytes 1179680 | tf_op jit(solution)/shard_map/all_to_all | solution.py:48
  117.2 1.9 %copy.48 = bf16[1,9,8,64,128]{4,3,1,2,0:T(8,128)(2,1)S(1)} copy(bf16[1,9,8,64,128]{4,1,3,2,0:T(8,128)(2,1)} %bitcast.118) | data formatting | bytes 2359296 | tf_op jit(solution)/shard_map/all_to_all | solution.py:48
  119.6 1.2 fusion.161
  120.8 1.8 %copy.34 = f32[8,9,64,128]{3,2,1,0:T(8,128)} copy(f32[8,9,64,128]{3,0,2,1:T(8,128)S(1)} %bitcast.521) | data formatting | bytes 4718592
  122.6 1.1 fusion.158
  123.9 1.1 fusion.159
  125.0 43.5 %all-reduce.4 = (f32[8,8]{1,0:T(8,128)S(1)}, f32[8,8]{1,0:T(8,128)S(1)}) all-reduce(f32[8,8]{1,0:T(8,128)S(1)} %fusion.158, f32[8,8]{1,0:T(8,128)S(1)} %fusion.159), channel_id=1, replica_groups=mesh['batch'=8,'chan'=4] {'batch','chan'}, use_global_device_ids=true, to_apply=%region_1.2 | all-reduce | flops 128 | bytes 1024 | tf_op jit(solution)/shard_map/psum | solution.py:80
  168.4 0.6 multiply_reduce_fusion.1
  169.0 0.6 multiply_reduce_fusion
  169.6 1.2 subtract_multiply_fusion.1
  170.8 1.2 subtract_multiply_fusion
  172.0 1.7 convert_convert_fusion
  173.6 1.5 convert_convert_fusion.1
  (78 shorter events, 10.6 us)
Async XLA Ops:
  7.2 2.1 %copy-start.20 = (f32[8,8]{1,0:T(8,128)S(1)}, f32[8,8]{1,0:T(8,128)}, u32[]{:S(2)}) copy-start(f32[8,8]{1,0:T(8,128)} %param.11) | copy-start | bytes 772
  11.6 4.4 %copy-start.8 = (bf16[8,9,64,128]{3,2,1,0:T(8,128)(2,1)S(1)}, bf16[8,9,64,128]{3,2,1,0:T(8,128)(2,1)}, u32[]{:S(2)}) copy-start(bf16[8,9,64,128]{3,2,1,0:T(8,128)(2,1)} %param.14) | copy-start | bytes 3538948
  11.6 24.0 %all-to-all-start = ((bf16[8,9,64,128]{3,2,1,0:T(8,128)(2,1)}), bf16[8,9,64,128]{3,2,1,0:T(8,128)(2,1)S(1)}, u32[]{:S(2)}, u32[]{:S(2)}) async-start(bf16[8,9,64,128]{3,2,1,0:T(8,128)(2,1)} %copy.24), calls=%async_computation | async-start | bytes 2359296 | tf_op jit(solution)/shard_map/all_to_all | solution.py:43
  16.0 1.0 copy-start.10
  16.0 1.3 copy-start.22
  21.7 0.8 copy-start.15
  21.7 1.0 copy-start.23
  23.9 0.7 copy-start.21
  29.5 1.3 copy-start.16
  29.5 1.3 copy-start.24
  31.4 3.0 %copy-start.11 = (bf16[1,32,32,128]{3,2,1,0:T(8,128)(2,1)S(1)}, bf16[1,32,32,128]{3,2,1,0:T(8,128)(2,1)}, u32[]{:S(2)}) copy-start(bf16[1,32,32,128]{3,2,1,0:T(8,128)(2,1)} %param.9) | copy-start | bytes 786436
  35.6 29.5 %all-to-all-start.1 = ((bf16[1,9,512,128]{3,1,0,2:T(8,128)(2,1)}), bf16[1,9,512,128]{3,1,0,2:T(8,128)(2,1)}, u32[]{:S(2)}, u32[]{:S(2)}) async-start(bf16[1,9,512,128]{3,1,0,2:T(8,128)(2,1)} %copy.27), calls=%async_computation.1 | async-start | bytes 4194304 | tf_op jit(solution)/shard_map/all_to_all | solution.py:48
  40.0 4.0 %copy-start.6 = (bf16[8,9,64,128]{3,2,0,1:T(8,128)(2,1)}, bf16[8,9,64,128]{3,2,0,1:T(8,128)(2,1)S(1)}, u32[]{:S(2)}) copy-start(bf16[8,9,64,128]{3,2,0,1:T(8,128)(2,1)S(1)} %copy.25) | copy-start | bytes 3538948
  65.1 21.4 %all-to-all-start.2 = ((bf16[8,9,64,128]{3,2,1,0:T(8,128)(2,1)}), bf16[8,9,64,128]{3,2,1,0:T(8,128)(2,1)}, u32[]{:S(2)}, u32[]{:S(2)}) async-start(bf16[8,9,64,128]{3,2,1,0:T(8,128)(2,1)} %copy.29), calls=%async_computation.2 | async-start | bytes 2359296 | tf_op jit(solution)/shard_map/all_to_all | solution.py:43
  75.5 2.9 %copy-start.14 = (bf16[1,32,32,128]{3,2,1,0:T(8,128)(2,1)S(1)}, bf16[1,32,32,128]{3,2,1,0:T(8,128)(2,1)}, u32[]{:S(2)}) copy-start(bf16[1,32,32,128]{3,2,1,0:T(8,128)(2,1)} %get-tuple-element.30) | copy-start | bytes 786436
  78.4 2.7 %copy-start.13 = (bf16[1,32,32,128]{3,2,1,0:T(8,128)(2,1)S(1)}, bf16[1,32,32,128]{3,2,1,0:T(8,128)(2,1)}, u32[]{:S(2)}) copy-start(bf16[1,32,32,128]{3,2,1,0:T(8,128)(2,1)} %get-tuple-element.35) | copy-start | bytes 786436
  81.1 2.7 %copy-start.12 = (bf16[1,32,32,128]{3,2,1,0:T(8,128)(2,1)S(1)}, bf16[1,32,32,128]{3,2,1,0:T(8,128)(2,1)}, u32[]{:S(2)}) copy-start(bf16[1,32,32,128]{3,2,1,0:T(8,128)(2,1)} %get-tuple-element.29) | copy-start | bytes 786436
  86.5 30.6 %all-to-all-start.3 = ((bf16[1,9,512,128]{3,1,0,2:T(8,128)(2,1)}), bf16[1,9,512,128]{3,1,0,2:T(8,128)(2,1)}, u32[]{:S(2)}, u32[]{:S(2)}) async-start(bf16[1,9,512,128]{3,1,0,2:T(8,128)(2,1)} %copy.31), calls=%async_computation.3 | async-start | bytes 4194304 | tf_op jit(solution)/shard_map/all_to_all | solution.py:48
  91.9 80.0 %all-reduce.8.cloned.1.call-start = ((), (), s32[]{:S(2)}) async-start(), calls=%async_computation.4 | async-start | bytes 2621440 | tf_op jit(solution)/shard_map/psum | solution.py:45
  91.9 10.2 %copy-start.4 = (f32[1024,512]{1,0:T(8,128)S(1)}, f32[1024,512]{1,0:T(8,128)}, u32[]{:S(2)}) copy-start(f32[1024,512]{1,0:T(8,128)} %fusion.128) | copy-start | bytes 6291460
  91.9 10.2 %copy-start.5 = (f32[1024,512]{1,0:T(8,128)S(1)}, f32[1024,512]{1,0:T(8,128)}, u32[]{:S(2)}) copy-start(f32[1024,512]{1,0:T(8,128)} %fusion.130) | copy-start | bytes 6291460
  94.6 5.1 %copy-start.19 = (bf16[1,16,16,128]{3,2,1,0:T(8,128)(2,1)S(1)}, bf16[1,16,16,128]{3,2,1,0:T(8,128)(2,1)}, u32[]{:S(2)}) copy-start(bf16[1,16,16,128]{3,2,1,0:T(8,128)(2,1)} %get-tuple-element.41) | copy-start | bytes 196612
  94.6 5.4 %copy-start.18 = (bf16[1,16,16,128]{3,2,1,0:T(8,128)(2,1)S(1)}, bf16[1,16,16,128]{3,2,1,0:T(8,128)(2,1)}, u32[]{:S(2)}) copy-start(bf16[1,16,16,128]{3,2,1,0:T(8,128)(2,1)} %get-tuple-element.42) | copy-start | bytes 196612
  95.7 2.5 %copy-start.17 = (bf16[1,16,16,128]{3,2,1,0:T(8,128)(2,1)S(1)}, bf16[1,16,16,128]{3,2,1,0:T(8,128)(2,1)}, u32[]{:S(2)}) copy-start(bf16[1,16,16,128]{3,2,1,0:T(8,128)(2,1)} %param.13) | copy-start | bytes 196612
  95.8 6.4 %copy-start.3 = (f32[1024,512]{1,0:T(8,128)S(1)}, f32[1024,512]{1,0:T(8,128)}, u32[]{:S(2)}) copy-start(f32[1024,512]{1,0:T(8,128)} %fusion.127) | copy-start | bytes 6291460
  97.0 5.2 %copy-start.2 = (f32[512,1024]{0,1:T(8,128)S(1)}, f32[512,1024]{0,1:T(8,128)}, u32[]{:S(2)}) copy-start(f32[512,1024]{0,1:T(8,128)} %fusion.126) | copy-start | bytes 6291460
  98.5 3.7 %copy-start.1 = (f32[1024,512]{1,0:T(8,128)S(1)}, f32[1024,512]{1,0:T(8,128)}, u32[]{:S(2)}) copy-start(f32[1024,512]{1,0:T(8,128)} %fusion.125) | copy-start | bytes 6291460
  100.0 2.2 %copy-start = (f32[1024,512]{1,0:T(8,128)S(1)}, f32[1024,512]{1,0:T(8,128)}, u32[]{:S(2)}) copy-start(f32[1024,512]{1,0:T(8,128)} %fusion.124) | copy-start | bytes 6291460
  120.8 1.8 %copy-start.7 = (bf16[8,9,64,128]{3,2,1,0:T(8,128)(2,1)S(1)}, bf16[8,9,64,128]{3,2,1,0:T(8,128)(2,1)}, u32[]{:S(2)}) copy-start(bf16[8,9,64,128]{3,2,1,0:T(8,128)(2,1)} %param.10) | copy-start | bytes 3538948
  122.6 1.3 copy-start.9
Sparse Core Ops, SparseCore 0:
  106.1 61.7 all-reduce.7
where the time goes:
time: 183 us; the launch traced here: 182 us
  matrix products  44.1 us (24%)
  blocking collectives  43.5 us (24%)
  waiting for transfers between devices  27.5 us (15%)
  local copies, waits for them, and re-layouts  26 us (14%)
  starting transfers between devices  19.8 us (11%)
  between operations  14.5 us (8%)
  other arithmetic  6.68 us (4%)
    psum x1, blocking collectives, per_device(): lax.psum((fine_partial, coarse_partial), ('batch', 'chan'))  43.5 us
    dot_general x18, matrix products, local_grads(): jnp.einsum('bpo,bco->bpc', window_up, kernels[:, tap], preferred_element_...  29 us
    all_to_all x2, waiting for transfers between devices, one_layer(): lax.all_to_all(kernel_grad.astype(jnp.bfloat16), 'batch', split_axis=2, c...  27.5 us
    all_to_all x2, starting transfers between devices, one_layer(): lax.all_to_all(mixed_all, 'batch', split_axis=0, concat_axis=2, tiled=True)  10 us
    all_to_all x2, starting transfers between devices, one_layer(): lax.all_to_all(kernel_grad.astype(jnp.bfloat16), 'batch', split_axis=2, c...  9.71 us
    dot_general x18, matrix products, local_grads(): jnp.einsum('bpc,bpo->bco', window_in, flat_up, preferred_element_type=jnp...  8.47 us
    unnamed x54, local copies, waits for them, and re-layouts  8.13 us
    all_to_all x2, local copies, waits for them, and re-layouts, one_layer(): lax.all_to_all(kernel_grad.astype(jnp.bfloat16), 'batch', split_axis=2, c...  4.92 us
  transfers between devices with their start and end apart: 5, of which 2 were waited for; matrix products, arithmetic and copies ran while one was open for 37% of the time, Pallas kernels for 0%

commit v1 on v0

--- a/solution.py
+++ b/solution.py
@@ -40,7 +40,12 @@
     flat_bank = bank_part.reshape(BANKS, -1).astype(jnp.float32)
     mixed_all = jnp.dot(coefs, flat_bank, precision=HIGH)
     mixed_all = mixed_all.reshape((coefs.shape[0],) + bank_part.shape[1:]).astype(jnp.bfloat16)
-    kernels = lax.all_to_all(mixed_all, "batch", split_axis=0, concat_axis=2, tiled=True)
+    kernels = jnp.concatenate(
+        lax.all_to_all(
+            jnp.stack(jnp.split(mixed_all, lax.axis_size("batch"), axis=0)), "batch", 0, 0
+        ),
+        axis=2,
+    )
     delta, kernel_grad = local_grads(inputs, upstream, kernels, side)
     delta_total = lax.psum(delta.astype(jnp.bfloat16), "chan").astype(jnp.float32)
     width = delta.shape[3] // lax.axis_size("chan")

time: 183 us -> 196 us (1.071)
  local copies, waits for them, and re-layouts: 26 us -> 39.4 us
  matrix products: 44.1 us -> 36.7 us
  waiting for transfers between devices: 27.5 us -> 33.1 us
    unnamed x54 -> x70, local copies, waits for them, and re-layouts: 8.13 us -> 19.7 us
    dot_general x18, matrix products: 29 us -> 22.7 us  [local_grads(): jnp.einsum('bpo,bco->bpc', window_up, kernels[:, tap], preferred_element_...]
    all_to_all x2, waiting for transfers between devices: 0.01 us -> 6.27 us  [one_layer(): lax.all_to_all(jnp.stack(jnp.split(mixed_all, lax.axis_size('batch'), axi...]
    split x0 -> x2, local copies, waits for them, and re-layouts: none -> 5.49 us  [one_layer(): jnp.split(mixed_all, lax.axis_size('batch'), axis=0)]
    convert_element_type x2 -> x0, local copies, waits for them, and re-layouts: 2.64 us -> none  [one_layer(): mixed_all.reshape((coefs.shape[0],) + bank_part.shape[1:])]
  transfers between devices with their start and end apart: 5 -> 5, of which waited for: 2 -> 3; matrix products, arithmetic and copies ran while one was open for 37% -> 33% of each run, Pallas kernels for 0% -> 0%
where the time goes in v1:
time: 196 us; the launch traced here: 194 us
  blocking collectives  43.6 us (22%)
  local copies, waits for them, and re-layouts  39.4 us (20%)
  matrix products  36.7 us (19%)
  waiting for transfers between devices  33.1 us (17%)
  starting transfers between devices  20.3 us (10%)
  between operations  14.4 us (7%)
  other arithmetic  6.16 us (3%)
    psum x1, blocking collectives, per_device(): lax.psum((fine_partial, coarse_partial), ('batch', 'chan'))  43.6 us
    all_to_all x2, waiting for transfers between devices, one_layer(): lax.all_to_all(kernel_grad.astype(jnp.bfloat16), 'batch', split_axis=2, c...  26.9 us
    dot_general x18, matrix products, local_grads(): jnp.einsum('bpo,bco->bpc', window_up, kernels[:, tap], preferred_element_...  22.7 us
    unnamed x70, local copies, waits for them, and re-layouts  19.7 us
    all_to_all x2, starting transfers between devices, one_layer(): lax.all_to_all(kernel_grad.astype(jnp.bfloat16), 'batch', split_axis=2, c...  11.5 us
    all_to_all x2, starting transfers between devices, one_layer(): lax.all_to_all(jnp.stack(jnp.split(mixed_all, lax.axis_size('batch'), axi...  8.81 us
    dot_general x18, matrix products, local_grads(): jnp.einsum('bpc,bpo->bco', window_in, flat_up, preferred_element_type=jnp...  7.39 us
    all_to_all x2, waiting for transfers between devices, one_layer(): lax.all_to_all(jnp.stack(jnp.split(mixed_all, lax.axis_size('batch'), axi...  6.27 us
  transfers between devices with their start and end apart: 5, of which 3 were waited for; matrix products, arithmetic and copies ran while one was open for 33% of the time, Pallas kernels for 0%

profile of v1, /device:TPU:10, one launch (start us, length us, event | category | flops | bytes accessed | tf_op | source)
XLA Modules:
  0.0 193.8 jit_solution(10969411023125886767)
XLA Ops:
  7.2 2.0 %copy.182 = bf16[1,8,576,128]{3,1,2,0:T(8,128)(2,1)S(1)} copy(bf16[1,8,576,128]{3,2,1,0:T(8,128)(2,1)} %bitcast.568) | data formatting | bytes 2359296
  9.2 1.1 convolution_convert_fusion.1
  10.3 2.7 %fusion.161 = (bf16[1,9,64,128]{3,0,2,1:T(2,128)(2,1)S(1)}, bf16[1,9,64,128]{3,0,2,1:T(2,128)(2,1)S(1)}, bf16[1,9,64,128]{3,0,2,1:T(2,128)(2,1)S(1)}, bf16[1,9,6...) fusion(bf16[8,9,64,128]{3,0,2,1:T(8,128)(2,1)S(1)} %convolution, ...), kind=kLoop, calls=%fused_computation.254 | loop fusion | bytes 2359296 | tf_op jit(solution)/shard_map/split | solution.py:45
  13.1 0.7 bitcast_dynamic-update-slice_fusion.15
  14.4 0.7 bitcast_dynamic-update-slice_fusion.13
  15.1 0.7 bitcast_dynamic-update-slice_fusion.12
  15.8 0.7 bitcast_dynamic-update-slice_fusion.11
  18.6 4.4 %all-to-all-start = ((bf16[8,1,9,64,128]{4,3,2,1,0:T(8,128)(2,1)}), bf16[8,1,9,64,128]{4,3,2,1,0:T(8,128)(2,1)S(1)}, u32[]{:S(2)}, u32[]{:S(2)}) async-start(bf16[8,1,9,64,128]{4,3,2,1,0:T(8,128)(2,1)} %bitcast_dynamic-update-slice_fusion.8), calls=%async_computation | async-start | bytes 2359296 | tf_op jit(solution)/shard_map/all_to_all | solution.py:44
  22.9 1.3 pad_slice_fusion.16
  24.8 0.8 copy.181
  25.6 1.1 convolution_convert_fusion
  26.7 2.7 %fusion.160 = (bf16[1,9,64,128]{3,0,2,1:T(2,128)(2,1)S(1)}, bf16[1,9,64,128]{3,0,2,1:T(2,128)(2,1)S(1)}, bf16[1,9,64,128]{3,0,2,1:T(2,128)(2,1)S(1)}, bf16[1,9,6...) fusion(bf16[8,9,64,128]{3,0,2,1:T(8,128)(2,1)S(1)} %convolution, ...), kind=kLoop, calls=%fused_computation.253 | loop fusion | bytes 2359296 | tf_op jit(solution)/shard_map/split | solution.py:45
  35.0 2.2 %copy.131 = bf16[1,9,512,128]{3,1,0,2:T(8,128)(2,1)} copy(bf16[1,9,512,128]{3,2,1,0:T(8,128)(2,1)S(1)} %fusion.62) | data formatting | bytes 2359296 | tf_op jit(solution)/shard_map/stack | solution.py:36
  39.8 2.2 %copy.134 = bf16[1,9,512,128]{3,1,0,2:T(8,128)(2,1)} copy(bf16[1,9,512,128]{3,2,1,0:T(8,128)(2,1)S(1)} %fusion.44) | data formatting | bytes 2359296 | tf_op jit(solution)/shard_map/stack | solution.py:36
  42.0 0.7 bitcast_dynamic-update-slice_fusion.6
  42.7 0.7 bitcast_dynamic-update-slice_fusion.5
  43.4 0.7 bitcast_dynamic-update-slice_fusion.4
  44.1 0.8 pad_slice_fusion.24
  45.6 0.7 bitcast_dynamic-update-slice_fusion.2
  47.6 4.4 %all-to-all-start.2 = ((bf16[8,1,9,64,128]{4,3,2,1,0:T(8,128)(2,1)}), bf16[8,1,9,64,128]{4,3,2,1,0:T(8,128)(2,1)}, u32[]{:S(2)}, u32[]{:S(2)}) async-start(bf16[8,1,9,64,128]{4,3,2,1,0:T(8,128)(2,1)} %bitcast_dynamic-update-slice_fusion), calls=%async_computation.2 | async-start | bytes 2359296 | tf_op jit(solution)/shard_map/all_to_all | solution.py:44
  52.2 0.8 copy-done.11
  54.0 1.7 fusion.124
  55.7 1.8 fusion.125
  57.5 1.8 fusion.126
  59.3 1.8 fusion.127
  61.1 6.3 %all-to-all-done.2 = bf16[8,1,9,64,128]{4,3,2,1,0:T(8,128)(2,1)} async-done(((bf16[8,1,9,64,128]{4,3,2,1,0:T(8,128)(2,1)}), bf16[8,1,9,64,128]{4,3,2,1,0:T(8,128)(2,1)}, u32[]{:S(2)}, u32[]{:S(2)}) %all-to-all-start.2) | async-done | bytes 1179680 | tf_op jit(solution)/shard_map/all_to_all | solution.py:44
  67.4 5.7 %all-to-all-start.1 = ((bf16[1,9,512,128]{3,1,0,2:T(8,128)(2,1)}), bf16[1,9,512,128]{3,1,0,2:T(8,128)(2,1)}, u32[]{:S(2)}, u32[]{:S(2)}) async-start(bf16[1,9,512,128]{3,1,0,2:T(8,128)(2,1)} %copy.131), calls=%async_computation.1 | async-start | bytes 4194304 | tf_op jit(solution)/shard_map/all_to_all | solution.py:53
  73.1 1.4 copy.133
  77.9 0.9 fusion.6
  78.9 1.8 fusion.128
  80.7 1.7 fusion.130
  82.4 1.7 fusion.129
  84.2 14.2 %all-to-all-done.1 = bf16[1,9,512,128]{3,1,0,2:T(8,128)(2,1)} async-done(((bf16[1,9,512,128]{3,1,0,2:T(8,128)(2,1)}), bf16[1,9,512,128]{3,1,0,2:T(8,128)(2,1)}, u32[]{:S(2)}, u32[]{:S(2)}) %all-to-all-start.1) | async-done | bytes 1179680 | tf_op jit(solution)/shard_map/all_to_all | solution.py:53
  98.4 5.8 %all-to-all-start.3 = ((bf16[1,9,512,128]{3,1,0,2:T(8,128)(2,1)}), bf16[1,9,512,128]{3,1,0,2:T(8,128)(2,1)}, u32[]{:S(2)}, u32[]{:S(2)}) async-start(bf16[1,9,512,128]{3,1,0,2:T(8,128)(2,1)} %copy.134), calls=%async_computation.3 | async-start | bytes 4194304 | tf_op jit(solution)/shard_map/all_to_all | solution.py:53
  104.1 7.1 %fusion.4 = bf16[1024,512]{1,0:T(8,128)(2,1)} fusion(f32[1024,512]{1,0:T(8,128)S(1)} %fusion.123, f32[1024,512]{1,0:T(8,128)} %fusion.124, f32[1024,512]{1,0:T(8,128)} %fusion.125, f32[512,1024]{0,1:T(8,128)} %fusion.126, f32[1024,512]{1,0:T(8,128)} %fusion.127, f32[1024,512]{1,0:T(8,128)} %fusion.128, f32[1024,512]{1,0:T(8,128)} %fusion.130, ...), kind=kOutput, calls=%fused_computation.5 | convolution fusion | flops 138936320 | bytes 18219008 | tf_op jit(solution)/shard_map/bpo,bco->bpc/dot_general | solution.py:33
  111.3 1.9 copy.184
  113.7 1.2 fusion.162
  114.9 1.8 copy.136
  116.7 12.7 %all-to-all-done.3 = bf16[1,9,512,128]{3,1,0,2:T(8,128)(2,1)} async-done(((bf16[1,9,512,128]{3,1,0,2:T(8,128)(2,1)}), bf16[1,9,512,128]{3,1,0,2:T(8,128)(2,1)}, u32[]{:S(2)}, u32[]{:S(2)}) %all-to-all-start.3) | async-done | bytes 1179680 | tf_op jit(solution)/shard_map/all_to_all | solution.py:53
  129.4 1.9 copy.183
  131.8 1.2 fusion.163
  133.0 1.8 copy.137
  134.8 1.1 fusion.158
  136.1 1.1 fusion.159
  137.2 43.6 %all-reduce.4 = (f32[8,8]{1,0:T(8,128)S(1)}, f32[8,8]{1,0:T(8,128)S(1)}) all-reduce(f32[8,8]{1,0:T(8,128)S(1)} %fusion.158, f32[8,8]{1,0:T(8,128)S(1)} %fusion.159), channel_id=1, replica_groups=mesh['batch'=8,'chan'=4] {'batch','chan'}, use_global_device_ids=true, to_apply=%region_1.2 | all-reduce | flops 128 | bytes 1024 | tf_op jit(solution)/shard_map/psum | solution.py:85
  182.0 1.8 subtract_multiply_fusion
  183.8 1.7 convert_convert_fusion
  185.5 1.5 convert_convert_fusion.1
  (95 shorter events, 20.2 us)
Async XLA Ops:
  7.2 2.1 %copy-start.22 = (f32[8,8]{1,0:T(8,128)S(1)}, f32[8,8]{1,0:T(8,128)}, u32[]{:S(2)}) copy-start(f32[8,8]{1,0:T(8,128)} %param.11) | copy-start | bytes 772
  18.6 4.4 %copy-start.3 = (bf16[1,32,32,128]{3,2,1,0:T(8,128)(2,1)S(1)}, bf16[1,32,32,128]{3,2,1,0:T(8,128)(2,1)}, u32[]{:S(2)}) copy-start(bf16[1,32,32,128]{3,2,1,0:T(8,128)(2,1)} %param.9) | copy-start | bytes 786436
  18.6 29.1 %all-to-all-start = ((bf16[8,1,9,64,128]{4,3,2,1,0:T(8,128)(2,1)}), bf16[8,1,9,64,128]{4,3,2,1,0:T(8,128)(2,1)S(1)}, u32[]{:S(2)}, u32[]{:S(2)}) async-start(bf16[8,1,9,64,128]{4,3,2,1,0:T(8,128)(2,1)} %bitcast_dynamic-update-slice_fusion.8), calls=%async_computation | async-start | bytes 2359296 | tf_op jit(solution)/shard_map/all_to_all | solution.py:44
  22.9 1.8 copy-start.1
  24.8 0.8 copy-start.23
  26.7 3.4 %copy-start.24 = (bf16[1,32,32,512]{3,2,1,0:T(8,128)(2,1)S(1)}, bf16[1,32,32,512]{3,2,1,0:T(8,128)(2,1)}, u32[]{:S(2)}) copy-start(bf16[1,32,32,512]{3,2,1,0:T(8,128)(2,1)} %param.8) | copy-start | bytes 3145732
  35.0 2.2 %copy-start.12 = (bf16[1,16,16,128]{3,2,1,0:T(8,128)(2,1)S(1)}, bf16[1,16,16,128]{3,2,1,0:T(8,128)(2,1)}, u32[]{:S(2)}) copy-start(bf16[1,16,16,128]{3,2,1,0:T(8,128)(2,1)} %param.13) | copy-start | bytes 196612
  35.0 2.2 %copy-start.25 = (bf16[1,16,16,512]{3,2,1,0:T(8,128)(2,1)S(1)}, bf16[1,16,16,512]{3,2,1,0:T(8,128)(2,1)}, u32[]{:S(2)}) copy-start(bf16[1,16,16,512]{3,2,1,0:T(8,128)(2,1)} %param.12) | copy-start | bytes 786436
  47.6 19.7 %all-to-all-start.2 = ((bf16[8,1,9,64,128]{4,3,2,1,0:T(8,128)(2,1)}), bf16[8,1,9,64,128]{4,3,2,1,0:T(8,128)(2,1)}, u32[]{:S(2)}, u32[]{:S(2)}) async-start(bf16[8,1,9,64,128]{4,3,2,1,0:T(8,128)(2,1)} %bitcast_dynamic-update-slice_fusion), calls=%async_computation.2 | async-start | bytes 2359296 | tf_op jit(solution)/shard_map/all_to_all | solution.py:44
  52.1 1.0 copy-start.11
  53.0 0.9 copy-start.10
  54.0 1.8 copy-start.9
  55.7 1.8 copy-start.4
  57.5 1.8 copy-start.8
  67.4 31.0 %all-to-all-start.1 = ((bf16[1,9,512,128]{3,1,0,2:T(8,128)(2,1)}), bf16[1,9,512,128]{3,1,0,2:T(8,128)(2,1)}, u32[]{:S(2)}, u32[]{:S(2)}) async-start(bf16[1,9,512,128]{3,1,0,2:T(8,128)(2,1)} %copy.131), calls=%async_computation.1 | async-start | bytes 4194304 | tf_op jit(solution)/shard_map/all_to_all | solution.py:53
  73.1 1.4 copy-start.20
  73.1 1.7 copy-start.19
  74.6 0.8 copy-start.18
  74.8 0.8 copy-start.17
  75.4 0.8 copy-start.13
  75.7 0.8 copy-start.16
  76.2 0.8 copy-start.15
  76.5 0.8 copy-start.14
  77.1 0.8 copy-start.21
  77.3 1.5 copy-start.7
  78.9 1.8 copy-start.6
  80.7 1.7 copy-start.5
  98.4 31.0 %all-to-all-start.3 = ((bf16[1,9,512,128]{3,1,0,2:T(8,128)(2,1)}), bf16[1,9,512,128]{3,1,0,2:T(8,128)(2,1)}, u32[]{:S(2)}, u32[]{:S(2)}) async-start(bf16[1,9,512,128]{3,1,0,2:T(8,128)(2,1)} %copy.134), calls=%async_computation.3 | async-start | bytes 4194304 | tf_op jit(solution)/shard_map/all_to_all | solution.py:53
  104.1 79.7 %all-reduce.8.cloned.1.call-start = ((), (), s32[]{:S(2)}) async-start(), calls=%async_computation.4 | async-start | bytes 2621440 | tf_op jit(solution)/shard_map/psum | solution.py:50
  133.0 1.8 copy-start
  134.8 1.3 copy-start.2
Sparse Core Ops, SparseCore 0:
  111.4 62.1 all-reduce.7
